TPU v7x, 256 devices: a whole 4x4x8 slice. The times are simulated.
256 devices in a mesh: section: 8 (over y, core), row: 32 (over z, x).
Axes of the slice: x: 4, y: 4, z: 8, core: 2. Of those that a mesh axis runs over, the one named last changes fastest.
Arguments:
- channel_rows_in: bfloat16 [1024, 32, 4096], P('row', None, 'section'), may hold values from -6 to 6
- gate_rows_in: bfloat16 [1024, 32, 4096], P('row', None, 'section'), may hold values from -6 to 6
- map_input_rows: bfloat16 [1024, 32, 256], P('row'), may hold values from -6 to 6
- step_size_input: bfloat16 [1024, 64, 32], P('row', 'section'), may hold values from -4 to 4
- channel_kernel_weight: float32 [4, 4096], P(None, 'section'), may hold values from -3 to 3
- map_kernel_weight: float32 [4, 256], replicated, may hold values from -3 to 3
- channel_conv_bias: float32 [4096], P('section'), may hold values from -3 to 3
- map_kernel_bias: float32 [256], replicated, may hold values from -3 to 3
- step_size_bias: float32 [64], P('section'), may hold values from -2 to 0
- head_decay_rate: float32 [64], P('section'), may hold values from 0.003 to 1
- head_skip_weight: float32 [64], P('section'), may hold values from 0.5 to 1.5
- gated_norm_scale: float32 [4096], P('section'), may hold values from 0.5 to 1.5
- scan_state_cache: bfloat16 [1024, 64, 64, 128], P('row', 'section'), may hold values from -2 to 2
- channel_window_cache: bfloat16 [1024, 3, 4096], P('row', None, 'section'), may hold values from -6 to 6
- map_window_cache: bfloat16 [1024, 3, 256], P('row'), may hold values from -6 to 6
- adapter_down_weight: bfloat16 [32, 64, 4096], P('row', None, 'section'), may hold values from -0.09375 to 0.09375
- adapter_up_weight: bfloat16 [32, 64, 4096], P('row', None, 'section'), may hold values from -0.75 to 0.75
- session_slot_index: int32 [1024], replicated, may hold values from 0 to 1023, as said below
- lengths: int32 [1024], replicated, may hold values from 1 to 32
- session_adapter_index: int32 [1024], replicated, may hold values from 0 to 31
Outputs:
- mixer_output_rows: bfloat16 [1024, 32, 4096], P('row', None, 'section')
- adapter_delta: bfloat16 [1024, 32, 4096], P('row', None, 'section')
- scan_state_next: bfloat16 [1024, 64, 64, 128], P('row', 'section')
- channel_window_next: bfloat16 [1024, 3, 4096], P('row', None, 'section')
- map_window_next: bfloat16 [1024, 3, 256], P('row')
Inputs may be any that keep to these rules, and one draw needn't show every extreme that they name: `session_slot_index`: A permutation of the 1024 cache slots; cache slot c lies on row c // 32 and served session q on row q // 32. The states of one serving row's sessions come from exactly 16 home rows, 2 from each, so every home row also sends to that many rows.
All inputs are finite; a program needn't handle non-finite values.
Results may differ from a plain program's by a relative error of at most 0.0058.
Values may be sent and summed in bfloat16 or wider, within the bound.
No kernel may reach another device: no remote copies, remote signals or barrier semaphores. Data moves between devices by JAX's collectives and lax.ppermute only.
A program may use at most 128 MiB of HBM per device.

v0:
```python
import jax
import jax.numpy as jnp
from jax import lax
from jax.sharding import PartitionSpec as P

INNER_CHANNELS = 4096
NORM_EPS = 1e-05


def sigmoid_linear(value):
    return value / (1.0 + jnp.exp(-value))


def conv_part(cached, fresh, weight, offset):
    extended = jnp.concatenate([cached.astype(jnp.float32), fresh.astype(jnp.float32)], axis=1)
    span_len = fresh.shape[1]
    summed = (
        offset + weight[0] * extended[:, 0:span_len] + weight[1] * extended[:, 1 : span_len + 1]
    )
    summed = (
        summed
        + weight[2] * extended[:, 2 : span_len + 2]
        + weight[3] * extended[:, 3 : span_len + 3]
    )
    return (sigmoid_linear(summed), extended)


def tail_state(extended, lengths):
    total_rows = extended.shape[1]
    picked = lengths[:, None] + jnp.arange(3, dtype=jnp.int32)[None, :]
    onehot = (picked[:, :, None] == jnp.arange(total_rows, dtype=jnp.int32)[None, None, :]).astype(
        jnp.float32
    )
    return jnp.einsum("skt,stc->skc", onehot, extended, precision=lax.Precision.HIGHEST).astype(
        jnp.bfloat16
    )


def mix_sessions(
    channel_rows_in,
    map_input_rows,
    step_size_input,
    lengths,
    scan_state_cache,
    channel_window_cache,
    map_window_cache,
    channel_kernel_weight,
    map_kernel_weight,
    channel_conv_bias,
    map_kernel_bias,
    step_size_bias,
    head_decay_rate,
    head_skip_weight,
):
    highest = lax.Precision.HIGHEST
    local_sess, span_len, channels = channel_rows_in.shape
    head_count = step_size_input.shape[1]
    head_dim = channels // head_count
    state_dim = map_input_rows.shape[2] // 2
    conv_x, ext_x = conv_part(
        channel_window_cache, channel_rows_in, channel_kernel_weight, channel_conv_bias
    )
    conv_m, ext_m = conv_part(map_window_cache, map_input_rows, map_kernel_weight, map_kernel_bias)
    valid = (jnp.arange(span_len, dtype=jnp.int32)[None, :] < lengths[:, None]).astype(jnp.float32)
    step_size = (
        jax.nn.softplus(step_size_input.astype(jnp.float32) + step_size_bias[None, :, None])
        * valid[:, None, :]
    )
    log_decay = jnp.cumsum(-head_decay_rate[None, :, None] * step_size, axis=2)
    input_map = conv_m[:, :, :state_dim]
    output_map = conv_m[:, :, state_dim:]
    x_heads = conv_x.reshape(local_sess, span_len, head_count, head_dim)
    per_block = max(1, 128 // span_len)
    block_count = local_sess // per_block
    block_rows = per_block * span_len
    owners = jnp.arange(block_rows) // span_len
    position = jnp.arange(block_rows)
    causal_mask = (owners[:, None] == owners[None, :]) & (position[:, None] >= position[None, :])
    decay_rows = jnp.transpose(log_decay, (0, 2, 1)).reshape(block_count, block_rows, head_count)
    decay_heads = jnp.transpose(decay_rows, (0, 2, 1))
    spread = decay_heads[:, :, :, None] - decay_heads[:, :, None, :]
    decay_mat = jnp.where(causal_mask, jnp.exp(jnp.where(causal_mask, spread, 0.0)), 0.0)
    in_rows = input_map.reshape(block_count, block_rows, state_dim)
    out_rows = output_map.reshape(block_count, block_rows, state_dim)
    scores = jnp.einsum("btn,bun->btu", out_rows, in_rows, precision=highest)
    step_rows = jnp.transpose(step_size, (0, 2, 1)).reshape(block_count, block_rows, head_count)
    scaled_x = (
        x_heads.reshape(block_count, block_rows, head_count, head_dim) * step_rows[:, :, :, None]
    )
    inside = jnp.einsum("bhtu,buhp->bthp", decay_mat * scores[:, None], scaled_x, precision=highest)
    inside = inside.reshape(local_sess, span_len, head_count, head_dim)
    state_old = scan_state_cache.astype(jnp.float32)
    carried = jnp.einsum("stn,shpn->sthp", output_map, state_old, precision=highest)
    carried = carried * jnp.exp(jnp.transpose(log_decay, (0, 2, 1)))[:, :, :, None]
    mixed_out = (inside + carried + head_skip_weight[None, None, :, None] * x_heads) * valid[
        :, :, None, None
    ]
    final_log = log_decay[:, :, -1]
    weights = jnp.exp(final_log[:, :, None] - log_decay) * step_size
    state_new = jnp.exp(final_log)[:, :, None, None] * state_old
    state_new = state_new + jnp.einsum(
        "sht,sthp,stn->shpn", weights, x_heads, input_map, precision=highest
    )
    return (
        mixed_out.reshape(local_sess, span_len, channels),
        state_new.astype(jnp.bfloat16),
        tail_state(ext_x, lengths),
        tail_state(ext_m, lengths),
    )


def pick_rows(source_rows, take_index, used_mask):
    row_total = source_rows.shape[0]
    onehot = (take_index[:, None] == jnp.arange(row_total, dtype=jnp.int32)[None, :]) & used_mask[
        :, None
    ]
    picked = jnp.dot(
        onehot.astype(source_rows.dtype),
        source_rows,
        preferred_element_type=jnp.float32,
        precision=lax.Precision.HIGHEST,
    )
    return picked.astype(source_rows.dtype)


def select_rows(source_rows, take_index):
    return pick_rows(source_rows, take_index, jnp.ones(take_index.shape, jnp.bool_))


def shards(
    channel_rows_in,
    gate_rows_in,
    map_input_rows,
    step_size_input,
    channel_kernel_weight,
    map_kernel_weight,
    channel_conv_bias,
    map_kernel_bias,
    step_size_bias,
    head_decay_rate,
    head_skip_weight,
    gated_norm_scale,
    scan_state_cache,
    channel_window_cache,
    map_window_cache,
    adapter_down_weight,
    adapter_up_weight,
    session_slot_index,
    lengths,
    session_adapter_index,
):
    local_sess = channel_rows_in.shape[0]
    row_count = lax.axis_size("row")
    row_index = lax.axis_index("row")
    capacity = max(2, 2 * local_sess // row_count)
    slot_count = row_count * capacity
    home_rows = (session_slot_index // local_sess).reshape(row_count, local_sess)
    same_home = home_rows[:, :, None] == home_rows[:, None, :]
    earlier = jnp.arange(local_sess)[None, :] < jnp.arange(local_sess)[:, None]
    rank_in_pair = (
        jnp.sum(jnp.where(same_home & earlier[None], 1, 0), axis=2).astype(jnp.int32).reshape(-1)
    )
    serve_rows = jnp.arange(row_count * local_sess, dtype=jnp.int32) // local_sess
    target = serve_rows * capacity + rank_in_pair
    source = session_slot_index // local_sess * capacity + rank_in_pair
    serve_slots = lax.dynamic_slice_in_dim(source, row_index * local_sess, local_sess)
    serve_lengths = lax.dynamic_slice_in_dim(lengths, row_index * local_sess, local_sess)
    serve_adapter = lax.dynamic_slice_in_dim(
        session_adapter_index, row_index * local_sess, local_sess
    )
    local_cache = jnp.arange(local_sess, dtype=jnp.int32) + row_index * local_sess
    cache_match = session_slot_index[None, :] == local_cache[:, None]
    home_slots = jnp.sum(jnp.where(cache_match, target[None, :], 0), axis=1)
    slot_range = jnp.arange(slot_count, dtype=jnp.int32)[:, None]
    local_range = jnp.arange(local_sess, dtype=jnp.int32)[None, :]
    home_fill = slot_range == home_slots[None, :]
    home_take = jnp.sum(jnp.where(home_fill, local_range, 0), axis=1)
    home_used = jnp.any(home_fill, axis=1)
    serve_fill = slot_range == serve_slots[None, :]
    serve_take = jnp.sum(jnp.where(serve_fill, local_range, 0), axis=1)
    serve_used = jnp.any(serve_fill, axis=1)
    layer_params = (
        channel_kernel_weight,
        map_kernel_weight,
        channel_conv_bias,
        map_kernel_bias,
        step_size_bias,
        head_decay_rate,
        head_skip_weight,
    )
    received = (
        lax.all_to_all(
            pick_rows(scan_state_cache.reshape(local_sess, -1), home_take, home_used),
            "row",
            split_axis=0,
            concat_axis=0,
            tiled=True,
        ),
        lax.all_to_all(
            pick_rows(channel_window_cache.reshape(local_sess, -1), home_take, home_used),
            "row",
            split_axis=0,
            concat_axis=0,
            tiled=True,
        ),
        lax.all_to_all(
            pick_rows(map_window_cache.reshape(local_sess, -1), home_take, home_used),
            "row",
            split_axis=0,
            concat_axis=0,
            tiled=True,
        ),
    )
    state_here = select_rows(received[0], serve_slots).reshape(scan_state_cache.shape)
    conv_here = select_rows(received[1], serve_slots).reshape(channel_window_cache.shape)
    map_here = select_rows(received[2], serve_slots).reshape(map_window_cache.shape)
    mixed, state_new, conv_new, map_new = mix_sessions(
        channel_rows_in,
        map_input_rows,
        step_size_input,
        serve_lengths,
        state_here,
        conv_here,
        map_here,
        *layer_params
    )
    returned = (
        lax.all_to_all(
            pick_rows(state_new.reshape(local_sess, -1), serve_take, serve_used),
            "row",
            split_axis=0,
            concat_axis=0,
            tiled=True,
        ),
        lax.all_to_all(
            pick_rows(conv_new.reshape(local_sess, -1), serve_take, serve_used),
            "row",
            split_axis=0,
            concat_axis=0,
            tiled=True,
        ),
        lax.all_to_all(
            pick_rows(map_new.reshape(local_sess, -1), serve_take, serve_used),
            "row",
            split_axis=0,
            concat_axis=0,
            tiled=True,
        ),
    )
    scan_state_next = select_rows(returned[0], home_slots).reshape(scan_state_cache.shape)
    channel_window_next = select_rows(returned[1], home_slots).reshape(channel_window_cache.shape)
    map_window_next = select_rows(returned[2], home_slots).reshape(map_window_cache.shape)
    gated = mixed * sigmoid_linear(gate_rows_in.astype(jnp.float32))
    square_sum = lax.psum(jnp.sum(gated * gated, axis=2), "section")
    inv_rms = lax.rsqrt(square_sum / INNER_CHANNELS + NORM_EPS)
    mixer_output_rows = (gated * inv_rms[:, :, None] * gated_norm_scale).astype(jnp.bfloat16)
    pieces = (
        lax.all_gather(adapter_down_weight, "row", axis=0, tiled=True),
        lax.all_gather(adapter_up_weight, "row", axis=0, tiled=True),
    )
    piece_len = pieces[0].shape[0]
    chosen = (serve_adapter[:, None] == jnp.arange(piece_len, dtype=jnp.int32)[None, :]).astype(
        jnp.bfloat16
    )
    down_part = jnp.einsum("sk,krc->src", chosen, pieces[0], preferred_element_type=jnp.float32)
    up_part = jnp.einsum("sk,krc->src", chosen, pieces[1], preferred_element_type=jnp.float32)
    low_part = jnp.einsum(
        "std,srd->str",
        mixer_output_rows,
        down_part.astype(jnp.bfloat16),
        preferred_element_type=jnp.float32,
    )
    low_total = lax.psum(low_part, "section").astype(jnp.bfloat16)
    adapter_delta = jnp.einsum(
        "str,src->stc", low_total, up_part.astype(jnp.bfloat16), preferred_element_type=jnp.float32
    ).astype(jnp.bfloat16)
    return (mixer_output_rows, adapter_delta, scan_state_next, channel_window_next, map_window_next)


def solution(mesh):
    return jax.shard_map(
        shards,
        mesh=mesh,
        in_specs=(
            P("row", None, "section"),
            P("row", None, "section"),
            P("row", None, None),
            P("row", "section", None),
            P(None, "section"),
            P(),
            P("section"),
            P(),
            P("section"),
            P("section"),
            P("section"),
            P("section"),
            P("row", "section", None, None),
            P("row", None, "section"),
            P("row", None, None),
            P("row", None, "section"),
            P("row", None, "section"),
            P(),
            P(),
            P(),
        ),
        out_specs=(
            P("row", None, "section"),
            P("row", None, "section"),
            P("row", "section", None, None),
            P("row", None, "section"),
            P("row", None, None),
        ),
        check_vma=False,
    )
```

profile of v0, /device:TPU:6, one launch (start us, length us, event | category | flops | bytes accessed | tf_op | source)
XLA Modules:
  0.0 662.8 jit_solution(1876397155071708182)
XLA Ops:
  12.7 11.6 %all-to-all-start.1 = ((bf16[32,2,768]{2,1,0:T(2,128)(2,1)}), bf16[32,2,768]{2,1,0:T(2,128)(2,1)S(1)}, u32[]{:S(2)}, u32[]{:S(2)}) async-start(bf16[32,2,768]{2,1,0:T(2,128)(2,1)} %all_to_all.51), calls=%async_computation.1 | async-start | bytes 196608 | tf_op jit(solution)/shard_map/all_to_all | solution.py:206
  26.2 6.7 %all-to-all-done.1 = bf16[32,2,768]{2,1,0:T(2,128)(2,1)S(1)} async-done(((bf16[32,2,768]{2,1,0:T(2,128)(2,1)}), bf16[32,2,768]{2,1,0:T(2,128)(2,1)S(1)}, u32[]{:S(2)}, u32[]{:S(2)}) %all-to-all-start.1) | async-done | bytes 98336 | tf_op jit(solution)/shard_map/all_to_all | solution.py:206
  32.9 5.4 all-to-all-start
  38.3 8.3 %convolution_convert_fusion.1 = bf16[64,65536]{1,0:T(8,128)(2,1)} fusion(bf16[4,8,512,128]{3,2,1,0:T(8,128)(2,1)} %bitcast.95, s32[64]{0:T(128)S(1)} %select_reduce_fusion.3, pred[64]{0:T(512)(128)(4,1)S(1)} %fusion.97), kind=kOutput, calls=%fused_computation.1 | convolution fusion | flops 272633856 | bytes 12583232 | tf_op jit(solution)/shard_map/dot_general | solution.py:117
  46.6 10.5 %all_to_all.54 = bf16[32,2,65536]{2,1,0:T(2,128)(2,1)} reshape(bf16[64,65536]{1,0:T(8,128)(2,1)} %convolution_convert_fusion.1) | data formatting | bytes 16777216 | tf_op jit(solution)/shard_map/all_to_all | solution.py:192
  57.1 10.4 %all-to-all-start.2 = ((bf16[32,2,65536]{2,1,0:T(2,128)(2,1)}), bf16[32,2,65536]{2,1,0:T(2,128)(2,1)}, u32[]{:S(2)}, u32[]{:S(2)}) async-start(bf16[32,2,65536]{2,1,0:T(2,128)(2,1)} %all_to_all.54), calls=%async_computation.2 | async-start | bytes 16777216 | tf_op jit(solution)/shard_map/all_to_all | solution.py:192
  68.7 5.9 reduce_window_sum.11
  83.5 4.7 add_divide_fusion
  95.1 4.3 broadcast_multiply_fusion
  99.4 153.6 %all-to-all-done.2 = bf16[32,2,65536]{2,1,0:T(2,128)(2,1)} async-done(((bf16[32,2,65536]{2,1,0:T(2,128)(2,1)}), bf16[32,2,65536]{2,1,0:T(2,128)(2,1)}, u32[]{:S(2)}, u32[]{:S(2)}) %all-to-all-start.2) | async-done | bytes 8388640 | tf_op jit(solution)/shard_map/all_to_all | solution.py:192
  253.0 9.6 %all-to-all-start.5 = ((bf16[32,2,768]{2,1,0:T(2,128)(2,1)}), bf16[32,2,768]{2,1,0:T(2,128)(2,1)S(1)}, u32[]{:S(2)}, u32[]{:S(2)}) async-start(bf16[32,2,768]{2,1,0:T(2,128)(2,1)} %all_to_all.63), calls=%async_computation.5 | async-start | bytes 196608 | tf_op jit(solution)/shard_map/all_to_all | solution.py:242
  262.6 10.2 %all_to_all.56 = bf16[64,65536]{1,0:T(8,128)(2,1)} reshape(bf16[32,2,65536]{2,1,0:T(2,128)(2,1)} %all-to-all-done.2) | data formatting | bytes 16777216 | tf_op jit(solution)/shard_map/all_to_all | solution.py:192
  272.8 4.7 fusion.19
  280.5 15.8 %add_convert_fusion = bf16[32,8,64,128]{3,2,1,0:T(8,128)(2,1)} fusion(bf16[32,8,64,128]{3,2,1,0:T(8,128)(2,1)S(1)} %bitcast.91, f32[32,8]{1,0:T(8,128)S(1)} %copy-done.15, f32[32,32,8,64]{3,2,1,0:T(8,128)S(1)} %copy-done.2, f32[32,32,256]{2,1,0:T(8,128)S(1)} %add_divide_fusion.1), kind=kOutput, calls=%fused_computation.4 | convolution fusion | flops 813694976 | bytes 13123584 | tf_op jit(solution)/shard_map/sht,sthp,stn->shpn/dot_general | solution.py:101
  296.9 9.8 %all-to-all-start.4 = ((bf16[32,2,1536]{2,1,0:T(2,128)(2,1)}), bf16[32,2,1536]{2,1,0:T(2,128)(2,1)S(1)}, u32[]{:S(2)}, u32[]{:S(2)}) async-start(bf16[32,2,1536]{2,1,0:T(2,128)(2,1)} %all_to_all.60), calls=%async_computation.4 | async-start | bytes 393216 | tf_op jit(solution)/shard_map/all_to_all | solution.py:235
  306.7 8.3 %convolution_convert_fusion = bf16[64,65536]{1,0:T(8,128)(2,1)} fusion(bf16[4,8,512,128]{3,2,1,0:T(8,128)(2,1)} %bitcast.93, s32[64]{0:T(128)S(1)} %copy-done.20, pred[64]{0:T(512)(128)(4,1)S(1)} %copy-done.22), kind=kOutput, calls=%fused_computation | convolution fusion | flops 272633856 | bytes 12583232 | tf_op jit(solution)/shard_map/dot_general | solution.py:117
  315.0 10.5 %all_to_all.57 = bf16[32,2,65536]{2,1,0:T(2,128)(2,1)} reshape(bf16[64,65536]{1,0:T(8,128)(2,1)} %convolution_convert_fusion) | data formatting | bytes 16777216 | tf_op jit(solution)/shard_map/all_to_all | solution.py:228
  325.6 9.8 %all-to-all-start.3 = ((bf16[32,2,65536]{2,1,0:T(2,128)(2,1)}), bf16[32,2,65536]{2,1,0:T(2,128)(2,1)}, u32[]{:S(2)}, u32[]{:S(2)}) async-start(bf16[32,2,65536]{2,1,0:T(2,128)(2,1)} %all_to_all.57), calls=%async_computation.3 | async-start | bytes 16777216 | tf_op jit(solution)/shard_map/all_to_all | solution.py:228
  347.2 3.7 broadcast_multiply_fusion.1
  350.9 8.9 %fusion.53 = f32[8,128,8,64]{1,3,2,0:T(8,128)S(1)} fusion(f32[8,128,128]{2,1,0:T(8,128)S(1)} %copy-done.10, f32[8,8,128]{2,1,0:T(8,128)S(1)} %copy.74, pred[128,128]{1,0:T(8,128)(4,1)S(1)} %fusion.79, f32[8,128,8,64]{3,2,1,0:T(8,128)S(1)} %broadcast_multiply_fusion.1), kind=kOutput, calls=%fused_computation.76 | convolution fusion | flops 809500672 | bytes 4767744 | tf_op jit(solution)/shard_map/bhtu,buhp->bthp/dot_general | solution.py:90
  364.6 87.1 %all-gather.5.cloned.1.call-done = bf16[32,64,512]{2,1,0:T(8,128)(2,1)} async-done(((bf16[1,64,512]{2,1,0:T(8,128)(2,1)}), bf16[32,64,512]{2,1,0:T(8,128)(2,1)}) %all-gather.5.cloned.1.call-update) | async-done | bytes 2097168 | tf_op jit(solution)/shard_map/all_gather | solution.py:259
  451.7 4.6 fusion.50
  456.3 92.9 %all-gather.3.cloned.1.call-done = bf16[32,64,512]{2,1,0:T(8,128)(2,1)} async-done(((bf16[1,64,512]{2,1,0:T(8,128)(2,1)}), bf16[32,64,512]{2,1,0:T(8,128)(2,1)}) %all-gather.3.cloned.1.call-update) | async-done | bytes 2097168 | tf_op jit(solution)/shard_map/all_gather | solution.py:258
  549.2 4.8 fusion.47
  553.9 13.9 %fusion.7 = f32[32,32,8,64]{3,1,2,0:T(8,128)S(1)} fusion(f32[32,32,8,64]{3,2,1,0:T(8,128)S(1)} %copy-done, f32[32,32,8,64]{3,2,1,0:T(8,128)} %bitcast.94, bf16[32,8,64,128]{3,2,1,0:T(8,128)(2,1)} %bitcast.92, f32[32,32]{1,0:T(8,128)S(1)} %fusion.104, f32[8]{0:T(128)S(1)} %copy-done.30, f32[32,32,8]{1,2,0:T(8,128)S(1)} %copy-done.8, ...), kind=kOutput, calls=%fused_computation.17 | convolution fusion | flops 807927808 | bytes 13255168 | tf_op jit(solution)/shard_map/stn,shpn->sthp/dot_general | solution.py:93
  567.9 5.8 copy.81
  573.7 3.5 reshape.245
  578.0 24.2 %psum.14 = f32[32,32]{1,0:T(8,128)S(1)} all-reduce(f32[32,32]{1,0:T(8,128)S(1)} %multiply_reduce_fusion), channel_id=1, replica_groups=mesh['section'=8,'row'=32] {'section'}, use_global_device_ids=true, to_apply=%region_6.7 | all-reduce | flops 1024 | bytes 8192 | tf_op jit(solution)/shard_map/psum | solution.py:254
  605.2 29.2 %all-reduce.1 = bf16[32,32,64]{2,1,0:T(8,128)(2,1)S(1)} all-reduce(f32[32,32,64]{2,1,0:T(8,128)S(1)} %fusion.38), channel_id=1, replica_groups=mesh['section'=8,'row'=32] {'section'}, use_global_device_ids=true, to_apply=%region_7.8 | all-reduce | flops 65536 | bytes 393216 | tf_op jit(solution)/shard_map/psum | solution.py:273
  634.3 3.6 fusion.58
  637.9 10.2 %all_to_all.59 = bf16[64,65536]{1,0:T(8,128)(2,1)} reshape(bf16[32,2,65536]{2,1,0:T(2,128)(2,1)} %all-to-all-done.3) | data formatting | bytes 16777216 | tf_op jit(solution)/shard_map/all_to_all | solution.py:228
  648.1 4.7 fusion.20
  (147 shorter events, 50.9 us)
Async XLA Ops:
  12.7 20.2 %all-to-all-start.1 = ((bf16[32,2,768]{2,1,0:T(2,128)(2,1)}), bf16[32,2,768]{2,1,0:T(2,128)(2,1)S(1)}, u32[]{:S(2)}, u32[]{:S(2)}) async-start(bf16[32,2,768]{2,1,0:T(2,128)(2,1)} %all_to_all.51), calls=%async_computation.1 | async-start | bytes 196608 | tf_op jit(solution)/shard_map/all_to_all | solution.py:206
  32.9 24.2 %all-to-all-start = ((bf16[32,2,1536]{2,1,0:T(2,128)(2,1)}), bf16[32,2,1536]{2,1,0:T(2,128)(2,1)S(1)}, u32[]{:S(2)}, u32[]{:S(2)}) async-start(bf16[32,2,1536]{2,1,0:T(2,128)(2,1)} %all_to_all.48), calls=%async_computation | async-start | bytes 393216 | tf_op jit(solution)/shard_map/all_to_all | solution.py:199
  57.1 10.5 %copy-start.31 = (f32[8]{0:T(128)S(1)}, f32[8]{0:T(128)}, u32[]{:S(2)}) copy-start(f32[8]{0:T(128)} %param.29) | copy-start | bytes 100
  57.1 11.4 %copy-start.13 = (bf16[32,8,32]{2,1,0:T(8,128)(2,1)S(1)}, bf16[32,8,32]{2,1,0:T(8,128)(2,1)}, u32[]{:S(2)}) copy-start(bf16[32,8,32]{2,1,0:T(8,128)(2,1)} %param.23) | copy-start | bytes 49156
  57.1 11.4 %copy-start.27 = (f32[8]{0:T(128)S(1)}, f32[8]{0:T(128)}, u32[]{:S(2)}) copy-start(f32[8]{0:T(128)} %param.28) | copy-start | bytes 100
  57.1 18.0 %copy-start.7 = (bf16[32,32,512]{2,1,0:T(8,128)(2,1)S(1)}, bf16[32,32,512]{2,1,0:T(8,128)(2,1)}, u32[]{:S(2)}) copy-start(bf16[32,32,512]{2,1,0:T(8,128)(2,1)} %param.20) | copy-start | bytes 3145732
  57.1 195.9 %all-to-all-start.2 = ((bf16[32,2,65536]{2,1,0:T(2,128)(2,1)}), bf16[32,2,65536]{2,1,0:T(2,128)(2,1)}, u32[]{:S(2)}, u32[]{:S(2)}) async-start(bf16[32,2,65536]{2,1,0:T(2,128)(2,1)} %all_to_all.54), calls=%async_computation.2 | async-start | bytes 16777216 | tf_op jit(solution)/shard_map/all_to_all | solution.py:192
  67.6 9.2 %copy-start.9 = (bf16[32,32,256]{2,1,0:T(8,128)(2,1)S(1)}, bf16[32,32,256]{2,1,0:T(8,128)(2,1)}, u32[]{:S(2)}) copy-start(bf16[32,32,256]{2,1,0:T(8,128)(2,1)} %param.22) | copy-start | bytes 1572868
  67.6 12.1 %copy-start.25 = (f32[4,256]{1,0:T(4,128)S(1)}, f32[4,256]{1,0:T(4,128)}, u32[]{:S(2)}) copy-start(f32[4,256]{1,0:T(4,128)} %param.25) | copy-start | bytes 12292
  67.6 12.1 %copy-start.18 = (f32[4,512]{1,0:T(4,128)S(1)}, f32[4,512]{1,0:T(4,128)}, u32[]{:S(2)}) copy-start(f32[4,512]{1,0:T(4,128)} %param.24) | copy-start | bytes 24580
  74.9 7.3 %copy-start.29 = (f32[256]{0:T(256)S(1)}, f32[256]{0:T(256)}, u32[]{:S(2)}) copy-start(f32[256]{0:T(256)} %param.27) | copy-start | bytes 3076
  76.8 6.7 %copy-start.23 = (s32[32]{0:T(128)}, s32[32]{0:T(128)S(1)}, u32[]{:S(2)}) copy-start(s32[32]{0:T(128)S(1)} %dynamic_slice.9) | copy-start | bytes 388
  79.6 3.5 copy-start.19
  79.7 3.4 copy-start.21
  253.0 43.3 %all-to-all-start.5 = ((bf16[32,2,768]{2,1,0:T(2,128)(2,1)}), bf16[32,2,768]{2,1,0:T(2,128)(2,1)S(1)}, u32[]{:S(2)}, u32[]{:S(2)}) async-start(bf16[32,2,768]{2,1,0:T(2,128)(2,1)} %all_to_all.63), calls=%async_computation.5 | async-start | bytes 196608 | tf_op jit(solution)/shard_map/all_to_all | solution.py:242
  262.6 10.2 %copy-start.24 = (s32[32]{0:T(128)S(1)}, s32[32]{0:T(128)}, u32[]{:S(2)}) copy-start(s32[32]{0:T(128)} %copy-done.23) | copy-start | bytes 388
  280.4 26.3 %copy-start.20 = (s32[64]{0:T(128)S(1)}, s32[64]{0:T(128)}, u32[]{:S(2)}) copy-start(s32[64]{0:T(128)} %copy-done.19) | copy-start | bytes 772
  280.4 26.3 %copy-start.22 = (pred[64]{0:T(512)(128)(4,1)S(1)}, pred[64]{0:T(512)(128)(4,1)}, u32[]{:S(2)}) copy-start(pred[64]{0:T(512)(128)(4,1)} %copy-done.21) | copy-start | bytes 196
  296.9 28.7 %all-to-all-start.4 = ((bf16[32,2,1536]{2,1,0:T(2,128)(2,1)}), bf16[32,2,1536]{2,1,0:T(2,128)(2,1)S(1)}, u32[]{:S(2)}, u32[]{:S(2)}) async-start(bf16[32,2,1536]{2,1,0:T(2,128)(2,1)} %all_to_all.60), calls=%async_computation.4 | async-start | bytes 393216 | tf_op jit(solution)/shard_map/all_to_all | solution.py:235
  325.6 312.3 %all-to-all-start.3 = ((bf16[32,2,65536]{2,1,0:T(2,128)(2,1)}), bf16[32,2,65536]{2,1,0:T(2,128)(2,1)}, u32[]{:S(2)}, u32[]{:S(2)}) async-start(bf16[32,2,65536]{2,1,0:T(2,128)(2,1)} %all_to_all.57), calls=%async_computation.3 | async-start | bytes 16777216 | tf_op jit(solution)/shard_map/all_to_all | solution.py:228
  335.4 116.3 %all-gather.5.cloned.1.call-start = ((), (), s32[]{:S(2)}) async-start(), calls=%async_computation.7 | async-start | bytes 2162688 | tf_op jit(solution)/shard_map/all_gather | solution.py:259
  336.2 213.0 %all-gather.3.cloned.1.call-start = ((), (), s32[]{:S(2)}) async-start(), calls=%async_computation.6 | async-start | bytes 2162688 | tf_op jit(solution)/shard_map/all_gather | solution.py:258
  347.2 3.7 copy-start.10
  359.8 3.0 copy-start.12
  359.8 3.0 copy-start.17
  359.8 91.9 %copy-start.28 = (s32[32]{0:T(128)S(1)}, s32[32]{0:T(128)}, u32[]{:S(2)}) copy-start(s32[32]{0:T(128)} %dynamic_slice.11) | copy-start | bytes 388
  364.6 189.4 %copy-start.8 = (f32[32,32,8]{1,2,0:T(8,128)S(1)}, f32[32,32,8]{1,2,0:T(8,128)}, u32[]{:S(2)}) copy-start(f32[32,32,8]{1,2,0:T(8,128)} %bitcast_exponential_fusion.1) | copy-start | bytes 98308
  364.6 189.4 %copy-start.30 = (f32[8]{0:T(128)S(1)}, f32[8]{0:T(128)}, u32[]{:S(2)}) copy-start(f32[8]{0:T(128)} %param.30) | copy-start | bytes 100
  549.2 4.8 copy-start
  573.7 3.5 copy-start.5
  573.7 28.5 %copy-start.26 = (f32[512]{0:T(512)S(1)}, f32[512]{0:T(512)}, u32[]{:S(2)}) copy-start(f32[512]{0:T(512)} %param.31) | copy-start | bytes 6148
  603.9 30.4 %copy-start.4 = (bf16[32,64,512]{2,0,1:T(8,128)(2,1)S(1)}, bf16[32,64,512]{2,0,1:T(8,128)(2,1)}, u32[]{:S(2)}) copy-start(bf16[32,64,512]{2,0,1:T(8,128)(2,1)} %fusion.50) | copy-start | bytes 6291460
  (8 other events, 12.7 us)
Sparse Core Ops, SparseCore 0:
  338.8 112.8 all-gather.4
  454.2 94.8 all-gather.2
where the time goes:
time: 669 us; the launch traced here: 663 us
  waiting for transfers between devices  341 us (51%)
  matrix products  86.7 us (13%)
  local copies, waits for them, and re-layouts  82.4 us (12%)
  starting transfers between devices  57.1 us (9%)
  blocking collectives  53.3 us (8%)
  other arithmetic  27.2 us (4%)
  between operations  14.8 us (2%)
    all_to_all x1, waiting for transfers between devices, shards(): lax.all_to_all(pick_rows(scan_state_cache.reshape(local_sess, -1), home_t...  154 us
    all_gather x1, waiting for transfers between devices, shards(): lax.all_gather(adapter_down_weight, 'row', axis=0, tiled=True)  92.9 us
    all_gather x1, waiting for transfers between devices, shards(): lax.all_gather(adapter_up_weight, 'row', axis=0, tiled=True)  87.1 us
    psum x1, blocking collectives, shards(): low_total = lax.psum(low_part, 'section').astype(jnp.bfloat16)  29.2 us
    dot_general x12, matrix products, pick_rows(): jnp.dot(onehot.astype(source_rows.dtype), source_rows, preferred_element_...  28.4 us
    psum x1, blocking collectives, shards(): square_sum = lax.psum(jnp.sum(gated * gated, axis=2), 'section')  24.2 us
    all_to_all x2, local copies, waits for them, and re-layouts, shards(): lax.all_to_all(pick_rows(scan_state_cache.reshape(local_sess, -1), home_t...  20.7 us
    all_to_all x2, local copies, waits for them, and re-layouts, shards(): lax.all_to_all(pick_rows(state_new.reshape(local_sess, -1), serve_take, s...  20.7 us
  transfers between devices with their start and end apart: 8, of which 4 were waited for; matrix products, arithmetic and copies ran while one was open for 20% of the time, Pallas kernels for 0%

commit v1 on v0

--- a/solution.py
+++ b/solution.py
@@ -256,7 +256,10 @@
     mixer_output_rows = (gated * inv_rms[:, :, None] * gated_norm_scale).astype(jnp.bfloat16)
     pieces = (
         lax.all_gather(adapter_down_weight, "row", axis=0, tiled=True),
-        lax.all_gather(adapter_up_weight, "row", axis=0, tiled=True),
+        jnp.concatenate(
+            lax.all_to_all(jnp.stack([adapter_up_weight] * lax.axis_size("row")), "row", 0, 0),
+            axis=0,
+        ),
     )
     piece_len = pieces[0].shape[0]
     chosen = (serve_adapter[:, None] == jnp.arange(piece_len, dtype=jnp.int32)[None, :]).astype(

time: 669 us -> 645 us (0.964)
  waiting for transfers between devices: 341 us -> 298 us
    all_gather x1 -> x0, waiting for transfers between devices: 87.1 us -> none  [shards(): lax.all_gather(adapter_up_weight, 'row', axis=0, tiled=True)]
    all_to_all x1, waiting for transfers between devices: 154 us -> 180 us  [shards(): lax.all_to_all(pick_rows(scan_state_cache.reshape(local_sess, -1), home_t...]
    all_gather x1, waiting for transfers between devices: 92.9 us -> 109 us  [shards(): lax.all_gather(adapter_down_weight, 'row', axis=0, tiled=True)]
    all_to_all x0 -> x1, starting transfers between devices: none -> 9.76 us  [shards(): lax.all_to_all(jnp.stack([adapter_up_weight] * lax.axis_size('row')), 'ro...]
  transfers between devices with their start and end apart: 8 -> 8, of which waited for: 4 -> 5; matrix products, arithmetic and copies ran while one was open for 20% -> 21% of each run, Pallas kernels for 0% -> 0%
where the time goes in v1:
time: 645 us; the launch traced here: 634 us
  waiting for transfers between devices  298 us (46%)
  local copies, waits for them, and re-layouts  87.4 us (14%)
  matrix products  85.3 us (13%)
  starting transfers between devices  62.7 us (10%)
  blocking collectives  56.6 us (9%)
  other arithmetic  29 us (4%)
  between operations  15.1 us (2%)
    all_to_all x1, waiting for transfers between devices, shards(): lax.all_to_all(pick_rows(scan_state_cache.reshape(local_sess, -1), home_t...  180 us
    all_gather x1, waiting for transfers between devices, shards(): lax.all_gather(adapter_down_weight, 'row', axis=0, tiled=True)  109 us
    dot_general x12, matrix products, pick_rows(): jnp.dot(onehot.astype(source_rows.dtype), source_rows, preferred_element_...  29.9 us
    psum x1, blocking collectives, shards(): low_total = lax.psum(low_part, 'section').astype(jnp.bfloat16)  29.2 us
    psum x1, blocking collectives, shards(): square_sum = lax.psum(jnp.sum(gated * gated, axis=2), 'section')  27.4 us
    all_to_all x2, local copies, waits for them, and re-layouts, shards(): lax.all_to_all(pick_rows(state_new.reshape(local_sess, -1), serve_take, s...  20.9 us
    all_to_all x2, local copies, waits for them, and re-layouts, shards(): lax.all_to_all(pick_rows(scan_state_cache.reshape(local_sess, -1), home_t...  20.8 us
    dot_general x1, matrix products, mix_sessions(): jnp.einsum('sht,sthp,stn->shpn', weights, x_heads, input_map, precision=h...  14.5 us
  transfers between devices with their start and end apart: 8, of which 5 were waited for; matrix products, arithmetic and copies ran while one was open for 21% of the time, Pallas kernels for 0%

profile of v1, /device:TPU:6, one launch (start us, length us, event | category | flops | bytes accessed | tf_op | source)
XLA Modules:
  0.0 634.1 jit_solution(7812461579881111198)
XLA Ops:
  12.7 11.6 %all-to-all-start.1 = ((bf16[32,2,768]{2,1,0:T(2,128)(2,1)}), bf16[32,2,768]{2,1,0:T(2,128)(2,1)S(1)}, u32[]{:S(2)}, u32[]{:S(2)}) async-start(bf16[32,2,768]{2,1,0:T(2,128)(2,1)} %all_to_all.54), calls=%async_computation.1 | async-start | bytes 196608 | tf_op jit(solution)/shard_map/all_to_all | solution.py:206
  32.9 6.9 %all-to-all-start = ((bf16[32,2,1536]{2,1,0:T(2,128)(2,1)}), bf16[32,2,1536]{2,1,0:T(2,128)(2,1)S(1)}, u32[]{:S(2)}, u32[]{:S(2)}) async-start(bf16[32,2,1536]{2,1,0:T(2,128)(2,1)} %all_to_all.51), calls=%async_computation | async-start | bytes 393216 | tf_op jit(solution)/shard_map/all_to_all | solution.py:199
  46.4 3.1 all-to-all-done
  49.4 6.8 %all-to-all-start.6 = ((bf16[32,2,768]{2,1,0:T(2,128)(2,1)}), bf16[32,2,768]{2,1,0:T(2,128)(2,1)}, u32[]{:S(2)}, u32[]{:S(2)}) async-start(bf16[32,2,768]{2,1,0:T(2,128)(2,1)} %all_to_all.67), calls=%async_computation.6 | async-start | bytes 196608 | tf_op jit(solution)/shard_map/all_to_all | solution.py:242
  64.9 7.6 %all-to-all-start.5 = ((bf16[32,2,1536]{2,1,0:T(2,128)(2,1)}), bf16[32,2,1536]{2,1,0:T(2,128)(2,1)S(1)}, u32[]{:S(2)}, u32[]{:S(2)}) async-start(bf16[32,2,1536]{2,1,0:T(2,128)(2,1)} %all_to_all.64), calls=%async_computation.5 | async-start | bytes 393216 | tf_op jit(solution)/shard_map/all_to_all | solution.py:235
  72.5 8.3 %convolution_convert_fusion.1 = bf16[64,65536]{1,0:T(8,128)(2,1)} fusion(bf16[4,8,512,128]{3,2,1,0:T(8,128)(2,1)} %bitcast.101, s32[64]{0:T(128)} %copy-done.28, pred[64]{0:T(512)(128)(4,1)} %copy-done.29), kind=kOutput, calls=%fused_computation.1 | convolution fusion | flops 272633856 | bytes 12583232 | tf_op jit(solution)/shard_map/dot_general | solution.py:117
  80.8 10.5 %all_to_all.57 = bf16[32,2,65536]{2,1,0:T(2,128)(2,1)} reshape(bf16[64,65536]{1,0:T(8,128)(2,1)} %convolution_convert_fusion.1) | data formatting | bytes 16777216 | tf_op jit(solution)/shard_map/all_to_all | solution.py:192
  92.1 9.8 %all-to-all-start.2 = ((bf16[32,2,65536]{2,1,0:T(2,128)(2,1)}), bf16[32,2,65536]{2,1,0:T(2,128)(2,1)}, u32[]{:S(2)}, u32[]{:S(2)}) async-start(bf16[32,2,65536]{2,1,0:T(2,128)(2,1)} %all_to_all.57), calls=%async_computation.2 | async-start | bytes 16777216 | tf_op jit(solution)/shard_map/all_to_all | solution.py:192
  102.1 180.3 %all-to-all-done.2 = bf16[32,2,65536]{2,1,0:T(2,128)(2,1)} async-done(((bf16[32,2,65536]{2,1,0:T(2,128)(2,1)}), bf16[32,2,65536]{2,1,0:T(2,128)(2,1)}, u32[]{:S(2)}, u32[]{:S(2)}) %all-to-all-start.2) | async-done | bytes 8388640 | tf_op jit(solution)/shard_map/all_to_all | solution.py:192
  284.0 9.8 %all-to-all-start.3 = ((bf16[32,1,64,512]{3,2,1,0:T(8,128)(2,1)}), bf16[32,1,64,512]{3,2,1,0:T(8,128)(2,1)}, u32[]{:S(2)}, u32[]{:S(2)}) async-start(bf16[32,1,64,512]{3,2,1,0:T(8,128)(2,1)} %stack.2), calls=%async_computation.3 | async-start | bytes 4194304 | tf_op jit(solution)/shard_map/all_to_all | solution.py:260
  293.9 5.9 reduce_window_sum.11
  304.6 4.6 add_divide_fusion
  311.7 4.2 broadcast_multiply_fusion
  316.0 10.2 %all_to_all.59 = bf16[64,65536]{1,0:T(8,128)(2,1)} reshape(bf16[32,2,65536]{2,1,0:T(2,128)(2,1)} %all-to-all-done.2) | data formatting | bytes 16777216 | tf_op jit(solution)/shard_map/all_to_all | solution.py:192
  326.2 4.7 fusion.19
  334.7 14.5 %add_convert_fusion = bf16[32,8,64,128]{3,2,1,0:T(8,128)(2,1)S(1)} fusion(bf16[32,8,64,128]{3,2,1,0:T(8,128)(2,1)S(1)} %bitcast.97, f32[32,8]{1,0:T(8,128)S(1)} %copy-done.17, f32[32,32,8,64]{3,2,1,0:T(8,128)S(1)} %copy-done.3, f32[32,32,256]{2,1,0:T(8,128)S(1)} %copy-done.4), kind=kOutput, calls=%fused_computation.4 | convolution fusion | flops 813694976 | bytes 13123584 | tf_op jit(solution)/shard_map/sht,sthp,stn->shpn/dot_general | solution.py:101
  349.2 6.1 convolution_convert_fusion
  355.3 10.6 %all_to_all.61 = bf16[32,2,65536]{2,1,0:T(2,128)(2,1)} reshape(bf16[64,65536]{1,0:T(8,128)(2,1)} %convolution_convert_fusion) | data formatting | bytes 16777216 | tf_op jit(solution)/shard_map/all_to_all | solution.py:228
  365.9 10.0 %all-to-all-start.4 = ((bf16[32,2,65536]{2,1,0:T(2,128)(2,1)}), bf16[32,2,65536]{2,1,0:T(2,128)(2,1)}, u32[]{:S(2)}, u32[]{:S(2)}) async-start(bf16[32,2,65536]{2,1,0:T(2,128)(2,1)} %all_to_all.61), calls=%async_computation.4 | async-start | bytes 16777216 | tf_op jit(solution)/shard_map/all_to_all | solution.py:228
  384.7 3.7 broadcast_multiply_fusion.1
  388.4 8.9 %fusion.54 = f32[8,128,8,64]{1,3,2,0:T(8,128)S(1)} fusion(f32[8,128,128]{2,1,0:T(8,128)S(1)} %copy-done.14, f32[8,8,128]{2,1,0:T(8,128)S(1)} %copy.96, pred[128,128]{1,0:T(8,128)(4,1)S(1)} %fusion.80, f32[8,128,8,64]{3,2,1,0:T(8,128)S(1)} %broadcast_multiply_fusion.1), kind=kOutput, calls=%fused_computation.77 | convolution fusion | flops 809500672 | bytes 4767744 | tf_op jit(solution)/shard_map/bhtu,buhp->bthp/dot_general | solution.py:90
  403.0 4.6 fusion.51
  407.6 109.3 %all-gather.2.cloned.1.call-done = bf16[32,64,512]{2,1,0:T(8,128)(2,1)} async-done(((bf16[1,64,512]{2,1,0:T(8,128)(2,1)}), bf16[32,64,512]{2,1,0:T(8,128)(2,1)}) %all-gather.2.cloned.1.call-update) | async-done | bytes 2097168 | tf_op jit(solution)/shard_map/all_gather | solution.py:258
  516.8 4.8 fusion.48
  521.7 13.9 %fusion.7 = f32[32,32,8,64]{3,1,2,0:T(8,128)S(1)} fusion(f32[32,32,8,64]{3,2,1,0:T(8,128)S(1)} %copy-done, f32[32,32,8,64]{3,2,1,0:T(8,128)} %bitcast.100, bf16[32,8,64,128]{3,2,1,0:T(8,128)(2,1)} %bitcast.98, f32[32,32]{1,0:T(8,128)S(1)} %fusion.105, f32[8]{0:T(128)S(1)} %copy-done.36, f32[32,32,8]{1,2,0:T(8,128)S(1)} %bitcast_exponential_fusion.1, ...), kind=kOutput, calls=%fused_computation.17 | convolution fusion | flops 807927808 | bytes 13255168 | tf_op jit(solution)/shard_map/stn,shpn->sthp/dot_general | solution.py:93
  535.6 5.8 copy.103
  541.4 3.5 reshape.251
  545.7 27.4 %psum.14 = f32[32,32]{1,0:T(8,128)S(1)} all-reduce(f32[32,32]{1,0:T(8,128)S(1)} %multiply_reduce_fusion), channel_id=1, replica_groups=mesh['section'=8,'row'=32] {'section'}, use_global_device_ids=true, to_apply=%region_6.7 | all-reduce | flops 1024 | bytes 8192 | tf_op jit(solution)/shard_map/psum | solution.py:254
  576.1 29.2 %all-reduce.1 = bf16[32,32,64]{2,1,0:T(8,128)(2,1)S(1)} all-reduce(f32[32,32,64]{2,1,0:T(8,128)S(1)} %fusion.39), channel_id=1, replica_groups=mesh['section'=8,'row'=32] {'section'}, use_global_device_ids=true, to_apply=%region_7.8 | all-reduce | flops 65536 | bytes 393216 | tf_op jit(solution)/shard_map/psum | solution.py:276
  605.3 3.6 fusion.59
  608.9 10.3 %all_to_all.63 = bf16[64,65536]{1,0:T(8,128)(2,1)} reshape(bf16[32,2,65536]{2,1,0:T(2,128)(2,1)} %all-to-all-done.4) | data formatting | bytes 16777216 | tf_op jit(solution)/shard_map/all_to_all | solution.py:228
  619.2 4.7 fusion.20
  (159 shorter events, 63.9 us)
Async XLA Ops:
  10.5 30.0 %copy-start.28 = (s32[64]{0:T(128)}, s32[64]{0:T(128)S(1)}, u32[]{:S(2)}) copy-start(s32[64]{0:T(128)S(1)} %select_reduce_fusion.3) | copy-start | bytes 772
  11.0 29.5 %copy-start.29 = (pred[64]{0:T(512)(128)(4,1)}, pred[64]{0:T(512)(128)(4,1)S(1)}, u32[]{:S(2)}) copy-start(pred[64]{0:T(512)(128)(4,1)S(1)} %fusion.98) | copy-start | bytes 196
  12.7 20.2 %all-to-all-start.1 = ((bf16[32,2,768]{2,1,0:T(2,128)(2,1)}), bf16[32,2,768]{2,1,0:T(2,128)(2,1)S(1)}, u32[]{:S(2)}, u32[]{:S(2)}) async-start(bf16[32,2,768]{2,1,0:T(2,128)(2,1)} %all_to_all.54), calls=%async_computation.1 | async-start | bytes 196608 | tf_op jit(solution)/shard_map/all_to_all | solution.py:206
  24.4 32.6 %copy-start.26 = (s32[32]{0:T(128)}, s32[32]{0:T(128)S(1)}, u32[]{:S(2)}) copy-start(s32[32]{0:T(128)S(1)} %dynamic_slice.9) | copy-start | bytes 388
  24.5 25.0 %copy-start.22 = (s32[64]{0:T(128)}, s32[64]{0:T(128)S(1)}, u32[]{:S(2)}) copy-start(s32[64]{0:T(128)S(1)} %select_reduce_fusion.2) | copy-start | bytes 772
  24.5 24.9 %copy-start.24 = (pred[64]{0:T(512)(128)(4,1)}, pred[64]{0:T(512)(128)(4,1)S(1)}, u32[]{:S(2)}) copy-start(pred[64]{0:T(512)(128)(4,1)S(1)} %fusion.94) | copy-start | bytes 196
  26.1 35.0 %copy-start.2 = (f32[32,32,512]{2,1,0:T(8,128)}, f32[32,32,512]{2,1,0:T(8,128)S(1)}, u32[]{:S(2)}) copy-start(f32[32,32,512]{2,1,0:T(8,128)S(1)} %convert_element_type.117) | copy-start | bytes 6291460
  30.0 27.0 %copy-start.33 = (s32[32]{0:T(128)}, s32[32]{0:T(128)S(1)}, u32[]{:S(2)}) copy-start(s32[32]{0:T(128)S(1)} %dynamic_slice.10) | copy-start | bytes 388
  32.9 16.5 %all-to-all-start = ((bf16[32,2,1536]{2,1,0:T(2,128)(2,1)}), bf16[32,2,1536]{2,1,0:T(2,128)(2,1)S(1)}, u32[]{:S(2)}, u32[]{:S(2)}) async-start(bf16[32,2,1536]{2,1,0:T(2,128)(2,1)} %all_to_all.51), calls=%async_computation | async-start | bytes 393216 | tf_op jit(solution)/shard_map/all_to_all | solution.py:199
  43.2 37.6 %copy-start.10 = (f32[32,3,256]{2,1,0:T(4,128)}, f32[32,3,256]{2,1,0:T(4,128)S(1)}, u32[]{:S(2)}) copy-start(f32[32,3,256]{2,1,0:T(4,128)S(1)} %reshape.260) | copy-start | bytes 294916
  49.4 15.5 %all-to-all-start.6 = ((bf16[32,2,768]{2,1,0:T(2,128)(2,1)}), bf16[32,2,768]{2,1,0:T(2,128)(2,1)}, u32[]{:S(2)}, u32[]{:S(2)}) async-start(bf16[32,2,768]{2,1,0:T(2,128)(2,1)} %all_to_all.67), calls=%async_computation.6 | async-start | bytes 196608 | tf_op jit(solution)/shard_map/all_to_all | solution.py:242
  64.9 26.5 %all-to-all-start.5 = ((bf16[32,2,1536]{2,1,0:T(2,128)(2,1)}), bf16[32,2,1536]{2,1,0:T(2,128)(2,1)S(1)}, u32[]{:S(2)}, u32[]{:S(2)}) async-start(bf16[32,2,1536]{2,1,0:T(2,128)(2,1)} %all_to_all.64), calls=%async_computation.5 | async-start | bytes 393216 | tf_op jit(solution)/shard_map/all_to_all | solution.py:235
  91.4 10.5 %copy-start.37 = (f32[8]{0:T(128)S(1)}, f32[8]{0:T(128)}, u32[]{:S(2)}) copy-start(f32[8]{0:T(128)} %param.29) | copy-start | bytes 100
  91.4 10.6 %copy-start.34 = (s32[32]{0:T(128)S(1)}, s32[32]{0:T(128)}, u32[]{:S(2)}) copy-start(s32[32]{0:T(128)} %copy-done.33) | copy-start | bytes 388
  91.4 190.9 %copy-start.18 = (bf16[1,64,512]{2,1,0:T(8,128)(2,1)S(1)}, bf16[1,64,512]{2,1,0:T(8,128)(2,1)}, u32[]{:S(2)}) copy-start(bf16[1,64,512]{2,1,0:T(8,128)(2,1)} %param.36) | copy-start | bytes 196612
  92.1 190.2 %all-to-all-start.2 = ((bf16[32,2,65536]{2,1,0:T(2,128)(2,1)}), bf16[32,2,65536]{2,1,0:T(2,128)(2,1)}, u32[]{:S(2)}, u32[]{:S(2)}) async-start(bf16[32,2,65536]{2,1,0:T(2,128)(2,1)} %all_to_all.57), calls=%async_computation.2 | async-start | bytes 16777216 | tf_op jit(solution)/shard_map/all_to_all | solution.py:192
  101.9 191.8 %copy-start.16 = (bf16[32,8,32]{2,1,0:T(8,128)(2,1)S(1)}, bf16[32,8,32]{2,1,0:T(8,128)(2,1)}, u32[]{:S(2)}) copy-start(bf16[32,8,32]{2,1,0:T(8,128)(2,1)} %param.23) | copy-start | bytes 49156
  102.0 191.8 %copy-start.32 = (f32[8]{0:T(128)S(1)}, f32[8]{0:T(128)}, u32[]{:S(2)}) copy-start(f32[8]{0:T(128)} %param.28) | copy-start | bytes 100
  282.3 20.5 %copy-start.30 = (f32[4,256]{1,0:T(4,128)S(1)}, f32[4,256]{1,0:T(4,128)}, u32[]{:S(2)}) copy-start(f32[4,256]{1,0:T(4,128)} %param.25) | copy-start | bytes 12292
  282.3 20.5 %copy-start.21 = (f32[4,512]{1,0:T(4,128)S(1)}, f32[4,512]{1,0:T(4,128)}, u32[]{:S(2)}) copy-start(f32[4,512]{1,0:T(4,128)} %param.24) | copy-start | bytes 24580
  282.3 20.6 %copy-start.11 = (f32[32,3,256]{2,1,0:T(4,128)S(1)}, f32[32,3,256]{2,1,0:T(4,128)}, u32[]{:S(2)}) copy-start(f32[32,3,256]{2,1,0:T(4,128)} %copy-done.10) | copy-start | bytes 294916
  282.4 20.6 %copy-start.35 = (f32[256]{0:T(256)S(1)}, f32[256]{0:T(256)}, u32[]{:S(2)}) copy-start(f32[256]{0:T(256)} %param.27) | copy-start | bytes 3076
  284.0 82.0 %all-to-all-start.3 = ((bf16[32,1,64,512]{3,2,1,0:T(8,128)(2,1)}), bf16[32,1,64,512]{3,2,1,0:T(8,128)(2,1)}, u32[]{:S(2)}, u32[]{:S(2)}) async-start(bf16[32,1,64,512]{3,2,1,0:T(8,128)(2,1)} %stack.2), calls=%async_computation.3 | async-start | bytes 4194304 | tf_op jit(solution)/shard_map/all_to_all | solution.py:260
  331.9 17.3 %copy-start.1 = (bf16[4,8,512,128]{3,2,1,0:T(8,128)(2,1)}, bf16[4,8,512,128]{3,2,1,0:T(8,128)(2,1)S(1)}, u32[]{:S(2)}) copy-start(bf16[4,8,512,128]{3,2,1,0:T(8,128)(2,1)S(1)} %copy.125) | copy-start | bytes 12582916
  334.7 14.5 %copy-start.23 = (s32[64]{0:T(128)S(1)}, s32[64]{0:T(128)}, u32[]{:S(2)}) copy-start(s32[64]{0:T(128)} %copy-done.22) | copy-start | bytes 772
  334.7 14.5 %copy-start.25 = (pred[64]{0:T(512)(128)(4,1)S(1)}, pred[64]{0:T(512)(128)(4,1)}, u32[]{:S(2)}) copy-start(pred[64]{0:T(512)(128)(4,1)} %copy-done.24) | copy-start | bytes 196
  365.9 12.2 %copy-start.15 = (f32[32,32,8]{1,2,0:T(8,128)S(1)}, f32[32,32,8]{1,2,0:T(8,128)}, u32[]{:S(2)}) copy-start(f32[32,32,8]{1,2,0:T(8,128)} %get-tuple-element.33) | copy-start | bytes 98308
  365.9 242.9 %all-to-all-start.4 = ((bf16[32,2,65536]{2,1,0:T(2,128)(2,1)}), bf16[32,2,65536]{2,1,0:T(2,128)(2,1)}, u32[]{:S(2)}, u32[]{:S(2)}) async-start(bf16[32,2,65536]{2,1,0:T(2,128)(2,1)} %all_to_all.61), calls=%async_computation.4 | async-start | bytes 16777216 | tf_op jit(solution)/shard_map/all_to_all | solution.py:228
  375.9 140.9 %all-gather.2.cloned.1.call-start = ((), (), s32[]{:S(2)}) async-start(), calls=%async_computation.7 | async-start | bytes 2162688 | tf_op jit(solution)/shard_map/all_gather | solution.py:258
  403.0 118.7 %copy-start.36 = (f32[8]{0:T(128)S(1)}, f32[8]{0:T(128)}, u32[]{:S(2)}) copy-start(f32[8]{0:T(128)} %param.30) | copy-start | bytes 100
  541.4 31.7 %copy-start.31 = (f32[512]{0:T(512)S(1)}, f32[512]{0:T(512)}, u32[]{:S(2)}) copy-start(f32[512]{0:T(512)} %param.31) | copy-start | bytes 6148
  574.8 30.4 %copy-start.6 = (bf16[32,64,512]{2,0,1:T(8,128)(2,1)S(1)}, bf16[32,64,512]{2,0,1:T(8,128)(2,1)}, u32[]{:S(2)}) copy-start(bf16[32,64,512]{2,0,1:T(8,128)(2,1)} %fusion.51) | copy-start | bytes 6291460
  (14 other events, 47.9 us)
Sparse Core Ops, SparseCore 0:
  379.3 137.4 all-gather.1
